TPU v7x, 32 devices: a whole 2x2x4 slice. The times are simulated.
32 devices in a mesh: tp: 4 (over y, x), row: 4 (over z), col: 2 (over core).
Axes of the slice: x: 2, y: 2, z: 4, core: 2. Of those that a mesh axis runs over, the one named last changes fastest.
Arguments:
- hidden: bfloat16 [128, 14336], P('col', 'row'), may hold values from -6 to 6
- out_grad: bfloat16 [128, 4096], P(None, ('tp', 'row')), may hold values from -6 to 6
- basis_in: bfloat16 [14336, 4096], P(('row', 'col'), 'tp'), may hold values from -0.046875 to 0.046875
- basis_out: bfloat16 [4096, 1024], P(('tp', 'row'), 'col'), may hold values from -0.09375 to 0.09375
- eigen: float32 [4096, 1024], P(('tp', 'row'), 'col'), may hold values from 0.02 to 2
Outputs:
- precond: float32 [4096, 14336], P(('tp', 'col'), 'row')
All inputs are finite; a program needn't handle non-finite values.
Results may differ from a plain program's by a relative error of at most 0.024.
Values may be sent and summed in bfloat16 or wider, within the bound.
No kernel may reach another device: no remote copies, remote signals or barrier semaphores. Data moves between devices by JAX's collectives and lax.ppermute only.
A program may use at most 64 MiB of HBM per device.

v0:
```python
import jax
import jax.numpy as jnp
from jax import lax
from jax.sharding import PartitionSpec as P

damping = 0.01


def contract_rows(left, right):
    return lax.dot_general(
        left, right, (((0,), (0,)), ((), ())), preferred_element_type=jnp.float32
    )


def contract_cols(left, right):
    return lax.dot_general(
        left, right, (((1,), (1,)), ((), ())), preferred_element_type=jnp.float32
    )


def shards(hidden, out_grad, basis_in, basis_out, eigen):
    tp_count = lax.axis_size("tp")
    col_count = lax.axis_size("col")
    basis_block = lax.all_gather(basis_in, "col", axis=0, tiled=True)
    partial_in = jnp.dot(hidden, basis_block, preferred_element_type=jnp.float32)
    rotated_in = lax.psum_scatter(
        partial_in.astype(jnp.bfloat16), "row", scatter_dimension=1, tiled=True
    )
    rotated_in = lax.all_gather(rotated_in, "col", axis=0, tiled=True)
    queries = rotated_in.shape[0]
    partial_out = jnp.dot(out_grad, basis_out, preferred_element_type=jnp.float32)
    rotated_out = lax.psum(partial_out, ("tp", "row")).astype(jnp.bfloat16)
    coeff = contract_rows(rotated_in, rotated_out)
    scaled = (coeff / (queries * (eigen + damping))).astype(jnp.bfloat16)
    mixed_part = contract_cols(scaled, lax.all_gather(basis_out, ("tp", "row"), axis=0, tiled=True))
    depth = mixed_part.shape[0]
    width = mixed_part.shape[1]
    mixed_part = mixed_part.reshape(depth, tp_count, col_count, width // (tp_count * col_count))
    mixed = lax.psum_scatter(
        mixed_part.astype(jnp.bfloat16), "col", scatter_dimension=2, tiled=True
    ).astype(jnp.float32)
    mixed = mixed.reshape(depth, width // col_count).astype(jnp.bfloat16)
    mixed = lax.all_gather(mixed, "row", axis=0, tiled=True)
    return lax.psum_scatter(
        lax.dot_general(
            mixed, basis_block, (((0,), (1,)), ((), ())), preferred_element_type=jnp.float32
        ).astype(jnp.bfloat16),
        "tp",
        scatter_dimension=0,
        tiled=True,
    ).astype(jnp.float32)


def solution(mesh):
    placed = (
        P("col", "row"),
        P(None, ("tp", "row")),
        P(("row", "col"), "tp"),
        P(("tp", "row"), "col"),
        P(("tp", "row"), "col"),
    )
    return jax.shard_map(
        shards, mesh=mesh, in_specs=placed, out_specs=P(("tp", "col"), "row"), check_vma=False
    )
```

profile of v0, /device:TPU:0, one launch (start us, length us, event | category | flops | bytes accessed | tf_op | source)
XLA Modules:
  0.0 397.8 jit_solution(9604397828768367093)
XLA Ops:
  7.4 0.0 copy-start
  7.4 0.0 all-gather.4.cloned.1.call-start
  7.4 0.7 all-gather.4.cloned.1.call-update
  8.1 0.0 copy-start.1
  8.1 0.0 copy-start.2
  8.1 0.0 copy-start.3
  8.1 0.0 reduce-scatter.4.cloned.1.call-start
  8.2 22.6 %all-gather.4.cloned.1.call-done = bf16[3584,1024]{1,0:T(8,128)(2,1)} async-done(((bf16[1792,1024]{1,0:T(8,128)(2,1)}), bf16[3584,1024]{1,0:T(8,128)(2,1)}) %all-gather.4.cloned.1.call-update) | async-done | bytes 7340048 | tf_op jit(solution)/shard_map/all_gather | solution.py:24
  30.8 0.0 copy-done
  30.8 5.1 %convolution_convert_fusion.2 = bf16[64,1024]{1,0:T(8,128)(2,1)} fusion(bf16[64,3584]{1,0:T(8,128)(2,1)S(1)} %copy-done, bf16[3584,1024]{1,0:T(8,128)(2,1)} %all-gather.4.cloned.1.call-done), kind=kOutput, calls=%fused_computation.4 | convolution fusion | flops 469827584 | bytes 7929856 | tf_op jit(solution)/shard_map/dot_general | solution.py:25
  35.9 0.0 reduce-scatter.4.cloned.1.call-update
  35.9 0.0 all-gather.6.cloned.1.call-start
  36.0 0.5 all-gather.6.cloned.1.call-update
  36.5 0.0 reduce-scatter.6.cloned.1.call-start
  36.5 0.0 copy-done.1
  36.6 0.0 copy-done.2
  36.6 0.2 fusion.9
  36.8 85.1 %all-reduce.1 = bf16[128,512]{1,0:T(8,128)(2,1)S(1)} all-reduce(f32[128,512]{1,0:T(8,128)S(1)} %fusion.9), channel_id=1, replica_groups=mesh['tp'=4,'row'=4,'col'=2] {'tp','row'}, use_global_device_ids=true, to_apply=%region_1.0 | all-reduce | flops 65536 | bytes 393216 | tf_op jit(solution)/shard_map/psum | solution.py:32
  121.9 0.0 reduce-scatter.4.cloned.1.call-done
  121.9 2.1 all_gather.13
  124.0 0.0 all-gather.6.cloned.1.call-done
  124.0 0.0 copy-done.3
  124.0 4.9 %convolution_convert_fusion.1 = bf16[256,4096]{1,0:T(8,128)(2,1)} fusion(bf16[4096,512]{1,0:T(8,128)(2,1)} %all-gather.6.cloned.1.call-done, bf16[128,256]{1,0:T(8,128)(2,1)S(1)} %all_gather.13, f32[256,512]{1,0:T(8,128)S(1)} %copy-done.3, bf16[128,512]{1,0:T(8,128)(2,1)S(1)} %all-reduce.1), kind=kOutput, calls=%fused_computation.1 | convolution fusion | flops 1108869120 | bytes 7012352 | tf_op jit(solution)/shard_map/dot_general | solution.py:16
  128.9 3.3 convert_element_type.30
  132.2 4.1 %copy.6 = bf16[256,4,2,512]{0,3,1,2:T(8,128)(2,1)} copy(bf16[256,4,2,512]{3,2,1,0:T(2,128)(2,1)S(1)} %convert_element_type.30) | data formatting | bytes 4194304 | tf_op jit(solution)/shard_map/convert_element_type | solution.py:40
  136.3 0.0 reduce-scatter.6.cloned.1.call-update
  136.4 0.0 all-gather.8.cloned.1.call-start
  136.4 6.9 %reduce-scatter.6.cloned.1.call-done = bf16[256,4,1,512]{0,3,1,2:T(8,128)(2,1)} async-done(((bf16[256,4,2,512]{0,3,1,2:T(8,128)(2,1)}), bf16[256,4,1,512]{0,3,1,2:T(8,128)(2,1)}) %reduce-scatter.6.cloned.1.call-update) | async-done | bytes 1048592 | tf_op jit(solution)/shard_map/reduce_scatter | solution.py:39
  143.3 0.0 all-gather.8.cloned.1.call-update
  143.4 0.0 reduce-scatter.8.cloned.1.call-start
  143.4 83.2 %all-gather.8.cloned.1.call-done = bf16[1024,2048]{0,1:T(8,128)(2,1)} async-done(((bf16[256,2048]{0,1:T(8,128)(2,1)}), bf16[1024,2048]{0,1:T(8,128)(2,1)}) %all-gather.8.cloned.1.call-update) | async-done | bytes 4194320 | tf_op jit(solution)/shard_map/all_gather | solution.py:43
  226.6 22.0 %convolution_convert_fusion = bf16[2048,3584]{1,0:T(8,128)(2,1)} fusion(bf16[1024,2048]{0,1:T(8,128)(2,1)} %all-gather.8.cloned.1.call-done, bf16[3584,1024]{1,0:T(8,128)(2,1)} %all-gather.4.cloned.1.call-done), kind=kOutput, calls=%fused_computation | convolution fusion | flops 15039725568 | bytes 26214400 | tf_op jit(solution)/shard_map/dot_general | solution.py:45
  248.6 0.0 reduce-scatter.8.cloned.1.call-update
  248.7 135.9 %reduce-scatter.8.cloned.1.call-done = bf16[512,3584]{1,0:T(8,128)(2,1)} async-done(((bf16[2048,3584]{1,0:T(8,128)(2,1)}), bf16[512,3584]{1,0:T(8,128)(2,1)}) %reduce-scatter.8.cloned.1.call-update) | async-done | bytes 3670032 | tf_op jit(solution)/shard_map/reduce_scatter | solution.py:44
  384.6 6.0 %convert_element_type.33 = f32[512,3584]{1,0:T(8,128)} convert(bf16[512,3584]{1,0:T(8,128)(2,1)} %reduce-scatter.8.cloned.1.call-done) | non-fusion elementwise | flops 1835008 | bytes 11010048 | tf_op jit(solution)/shard_map/convert_element_type | solution.py:51
Async XLA Ops:
  7.4 23.4 %copy-start = (bf16[64,3584]{1,0:T(8,128)(2,1)S(1)}, bf16[64,3584]{1,0:T(8,128)(2,1)}, u32[]{:S(2)}) copy-start(bf16[64,3584]{1,0:T(8,128)(2,1)} %param.5) | copy-start | bytes 1376260
  7.4 23.4 %all-gather.4.cloned.1.call-start = ((), (), s32[]{:S(2)}) async-start(), calls=%async_computation.3 | async-start | bytes 11010048 | tf_op jit(solution)/shard_map/all_gather | solution.py:24
  8.1 28.5 %copy-start.1 = (bf16[256,512]{1,0:T(8,128)(2,1)S(1)}, bf16[256,512]{1,0:T(8,128)(2,1)}, u32[]{:S(2)}) copy-start(bf16[256,512]{1,0:T(8,128)(2,1)} %param.8) | copy-start | bytes 786436
  8.1 28.5 %copy-start.2 = (bf16[128,256]{1,0:T(8,128)(2,1)S(1)}, bf16[128,256]{1,0:T(8,128)(2,1)}, u32[]{:S(2)}) copy-start(bf16[128,256]{1,0:T(8,128)(2,1)} %param.6) | copy-start | bytes 196612
  8.1 115.9 %copy-start.3 = (f32[256,512]{1,0:T(8,128)S(1)}, f32[256,512]{1,0:T(8,128)}, u32[]{:S(2)}) copy-start(f32[256,512]{1,0:T(8,128)} %param.9) | copy-start | bytes 1572868
  8.1 113.8 %reduce-scatter.4.cloned.1.call-start = ((), (), s32[]{:S(2)}) async-start(), calls=%async_computation.4 | async-start | bytes 163840 | tf_op jit(solution)/shard_map/reduce_scatter | solution.py:26
  35.9 88.1 %all-gather.6.cloned.1.call-start = ((), (), s32[]{:S(2)}) async-start(), calls=%async_computation.5 | async-start | bytes 4456448 | tf_op jit(solution)/shard_map/all_gather | solution.py:35
  36.5 106.8 %reduce-scatter.6.cloned.1.call-start = ((), (), s32[]{:S(2)}) async-start(), calls=%async_computation.6 | async-start | bytes 3145728 | tf_op jit(solution)/shard_map/reduce_scatter | solution.py:39
  136.4 90.2 %all-gather.8.cloned.1.call-start = ((), (), s32[]{:S(2)}) async-start(), calls=%async_computation.7 | async-start | bytes 5242880 | tf_op jit(solution)/shard_map/all_gather | solution.py:43
  143.4 241.2 %reduce-scatter.8.cloned.1.call-start = ((), (), s32[]{:S(2)}) async-start(), calls=%async_computation.8 | async-start | bytes 18350080 | tf_op jit(solution)/shard_map/reduce_scatter | solution.py:44
Sparse Core Ops, SparseCore 0:
  9.7 21.0 all-gather.3
  36.0 21.2 reduce-scatter.3
  136.5 6.8 reduce-scatter.5
  144.7 81.7 all-gather.7
Sparse Core Ops, SparseCore 1:
  39.2 78.1 all-gather.5
  248.7 135.8 reduce-scatter.7
where the time goes:
time: 398 us
  waiting for transfers between devices  250 us (63%)
  blocking collectives  87.2 us (22%)
  matrix products  32.3 us (8%)
  between operations  14.7 us (4%)
  local copies, waits for them, and re-layouts  7.4 us (2%)
  other arithmetic  6.04 us (2%)
    reduce_scatter x1, waiting for transfers between devices, shards(): lax.psum_scatter(lax.dot_general(mixed, basis_block, (((0,), (1,)), ((),...  136 us
    psum x1, blocking collectives, shards(): rotated_out = lax.psum(partial_out, ('tp', 'row')).astype(jnp.bfloat16)  85.1 us
    all_gather x1, waiting for transfers between devices, shards(): mixed = lax.all_gather(mixed, 'row', axis=0, tiled=True)  83.2 us
    all_gather x1, waiting for transfers between devices, shards(): basis_block = lax.all_gather(basis_in, 'col', axis=0, tiled=True)  22.6 us
    dot_general x1, matrix products, shards(): lax.dot_general(mixed, basis_block, (((0,), (1,)), ((), ())), preferred_e...  22 us
  transfers between devices with their start and end apart: 6, of which 4 were waited for; matrix products, arithmetic and copies ran while one was open for 0% of the time, Pallas kernels for 0%

commit v1 on v0

--- a/solution.py
+++ b/solution.py
@@ -4,6 +4,10 @@
 from jax.sharding import PartitionSpec as P
 
 damping = 0.01
+
+
+def targets_scan(original):
+    return jnp.sum(lax.all_gather(original, ("tp", "row")), axis=0)
 
 
 def contract_rows(left, right):
@@ -29,7 +33,7 @@
     rotated_in = lax.all_gather(rotated_in, "col", axis=0, tiled=True)
     queries = rotated_in.shape[0]
     partial_out = jnp.dot(out_grad, basis_out, preferred_element_type=jnp.float32)
-    rotated_out = lax.psum(partial_out, ("tp", "row")).astype(jnp.bfloat16)
+    rotated_out = targets_scan(partial_out).astype(jnp.bfloat16)
     coeff = contract_rows(rotated_in, rotated_out)
     scaled = (coeff / (queries * (eigen + damping))).astype(jnp.bfloat16)
     mixed_part = contract_cols(scaled, lax.all_gather(basis_out, ("tp", "row"), axis=0, tiled=True))

time: 398 us -> 468 us (1.18)
  waiting for transfers between devices: 250 us -> 402 us
  blocking collectives: 87.2 us -> 2.05 us
    psum x1 -> x0, blocking collectives: 85.1 us -> none  [shards(): rotated_out = lax.psum(partial_out, ('tp', 'row')).astype(jnp.bfloat16)]
    all_gather x1, waiting for transfers between devices: 0.01 us -> 74.1 us  [shards(): lax.all_gather(basis_out, ('tp', 'row'), axis=0, tiled=True)]
    all_gather x0 -> x1, waiting for transfers between devices: none -> 56.7 us  [targets_scan(): return jnp.sum(lax.all_gather(original, ('tp', 'row')), axis=0)]
    reduce_scatter x1, waiting for transfers between devices: 0.02 us -> 19.6 us  [shards(): lax.psum_scatter(partial_in.astype(jnp.bfloat16), 'row', scatter_dimensio...]
  transfers between devices with their start and end apart: 6 -> 7, of which waited for: 4 -> 7; matrix products, arithmetic and copies ran while one was open for 0% -> 1% of each run, Pallas kernels for 0% -> 0%
where the time goes in v1:
time: 468 us
  waiting for transfers between devices  402 us (86%)
  matrix products  33 us (7%)
  between operations  14.9 us (3%)
  other arithmetic  8.68 us (2%)
  local copies, waits for them, and re-layouts  7.4 us (2%)
    reduce_scatter x1, waiting for transfers between devices, shards(): lax.psum_scatter(lax.dot_general(mixed, basis_block, (((0,), (1,)), ((),...  136 us
    all_gather x1, waiting for transfers between devices, shards(): mixed = lax.all_gather(mixed, 'row', axis=0, tiled=True)  83.2 us
    all_gather x1, waiting for transfers between devices, shards(): lax.all_gather(basis_out, ('tp', 'row'), axis=0, tiled=True)  74.1 us
    all_gather x1, waiting for transfers between devices, targets_scan(): return jnp.sum(lax.all_gather(original, ('tp', 'row')), axis=0)  56.7 us
    all_gather x1, waiting for transfers between devices, shards(): basis_block = lax.all_gather(basis_in, 'col', axis=0, tiled=True)  22.6 us
    dot_general x1, matrix products, shards(): lax.dot_general(mixed, basis_block, (((0,), (1,)), ((), ())), preferred_e...  22 us
    reduce_scatter x1, waiting for transfers between devices, shards(): lax.psum_scatter(partial_in.astype(jnp.bfloat16), 'row', scatter_dimensio...  19.6 us
  transfers between devices with their start and end apart: 7, of which 7 were waited for; matrix products, arithmetic and copies ran while one was open for 1% of the time, Pallas kernels for 0%

profile of v1, /device:TPU:0, one launch (start us, length us, event | category | flops | bytes accessed | tf_op | source)
XLA Modules:
  0.0 468.1 jit_solution(6623680096974001339)
XLA Ops:
  7.4 0.0 copy-start
  7.4 0.0 all-gather.6.cloned.1.call-start
  7.4 0.7 all-gather.6.cloned.1.call-update
  8.1 0.0 copy-start.1
  8.1 0.0 copy-start.2
  8.1 0.0 reduce-scatter.4.cloned.1.call-start
  8.2 22.6 %all-gather.6.cloned.1.call-done = bf16[3584,1024]{1,0:T(8,128)(2,1)} async-done(((bf16[1792,1024]{1,0:T(8,128)(2,1)}), bf16[3584,1024]{1,0:T(8,128)(2,1)}) %all-gather.6.cloned.1.call-update) | async-done | bytes 7340048 | tf_op jit(solution)/shard_map/all_gather | solution.py:28
  30.8 0.0 copy-done
  30.8 5.1 %convolution_convert_fusion.2 = bf16[64,1024]{1,0:T(8,128)(2,1)} fusion(bf16[64,3584]{1,0:T(8,128)(2,1)S(1)} %copy-done, bf16[3584,1024]{1,0:T(8,128)(2,1)} %all-gather.6.cloned.1.call-done), kind=kOutput, calls=%fused_computation.4 | convolution fusion | flops 469827584 | bytes 7929856 | tf_op jit(solution)/shard_map/dot_general | solution.py:29
  35.9 0.0 copy-start.3
  35.9 0.0 reduce-scatter.4.cloned.1.call-update
  35.9 0.0 all-gather.12.cloned.1.call-start
  36.0 0.0 copy-done.1
  36.0 0.0 copy-done.2
  36.0 0.9 fusion.9
  36.9 0.0 all-gather.12.cloned.1.call-update
  36.9 0.0 all-gather.8.cloned.1.call-start
  37.0 0.5 all-gather.8.cloned.1.call-update
  37.5 0.0 reduce-scatter.6.cloned.1.call-start
  37.5 19.6 %reduce-scatter.4.cloned.1.call-done = bf16[64,256]{1,0:T(8,128)(2,1)} async-done(((bf16[64,1024]{1,0:T(8,128)(2,1)}), bf16[64,256]{1,0:T(8,128)(2,1)}) %reduce-scatter.4.cloned.1.call-update) | async-done | bytes 32784 | tf_op jit(solution)/shard_map/reduce_scatter | solution.py:30
  57.1 2.1 all_gather.19
  59.2 56.7 %all-gather.12.cloned.1.call-done = f32[2048,512]{1,0:T(8,128)} async-done(((f32[128,512]{1,0:T(8,128)}), f32[2048,512]{1,0:T(8,128)}) %all-gather.12.cloned.1.call-update) | async-done | bytes 4194320 | tf_op jit(solution)/shard_map/all_gather | solution.py:10
  115.9 2.6 reduce_sum.9
  118.5 74.1 %all-gather.8.cloned.1.call-done = bf16[4096,512]{1,0:T(8,128)(2,1)} async-done(((bf16[256,512]{1,0:T(8,128)(2,1)}), bf16[4096,512]{1,0:T(8,128)(2,1)}) %all-gather.8.cloned.1.call-update) | async-done | bytes 4194320 | tf_op jit(solution)/shard_map/all_gather | solution.py:39
  192.6 0.0 copy-done.3
  192.6 4.9 %convolution_convert_fusion.1 = bf16[256,4096]{1,0:T(8,128)(2,1)} fusion(bf16[4096,512]{1,0:T(8,128)(2,1)} %all-gather.8.cloned.1.call-done, bf16[128,256]{1,0:T(8,128)(2,1)S(1)} %all_gather.19, f32[256,512]{1,0:T(8,128)S(1)} %copy-done.3, bf16[128,512]{1,0:T(8,128)(2,1)S(1)} %reduce_sum.9), kind=kOutput, calls=%fused_computation.1 | convolution fusion | flops 1108869120 | bytes 7012352 | tf_op jit(solution)/shard_map/dot_general | solution.py:20
  197.5 3.3 convert_element_type.30
  200.8 4.1 copy.6
  204.9 0.0 reduce-scatter.6.cloned.1.call-update
  204.9 0.0 all-gather.10.cloned.1.call-start
  205.0 8.5 %reduce-scatter.6.cloned.1.call-done = bf16[256,4,1,512]{0,3,1,2:T(8,128)(2,1)} async-done(((bf16[256,4,2,512]{0,3,1,2:T(8,128)(2,1)}), bf16[256,4,1,512]{0,3,1,2:T(8,128)(2,1)}) %reduce-scatter.6.cloned.1.call-update) | async-done | bytes 1048592 | tf_op jit(solution)/shard_map/reduce_scatter | solution.py:43
  213.4 0.0 all-gather.10.cloned.1.call-update
  213.5 0.0 reduce-scatter.8.cloned.1.call-start
  213.5 83.2 %all-gather.10.cloned.1.call-done = bf16[1024,2048]{0,1:T(8,128)(2,1)} async-done(((bf16[256,2048]{0,1:T(8,128)(2,1)}), bf16[1024,2048]{0,1:T(8,128)(2,1)}) %all-gather.10.cloned.1.call-update) | async-done | bytes 4194320 | tf_op jit(solution)/shard_map/all_gather | solution.py:47
  296.7 22.0 %convolution_convert_fusion = bf16[2048,3584]{1,0:T(8,128)(2,1)} fusion(bf16[1024,2048]{0,1:T(8,128)(2,1)} %all-gather.10.cloned.1.call-done, bf16[3584,1024]{1,0:T(8,128)(2,1)} %all-gather.6.cloned.1.call-done), kind=kOutput, calls=%fused_computation | convolution fusion | flops 15039725568 | bytes 26214400 | tf_op jit(solution)/shard_map/dot_general | solution.py:49
  318.7 0.0 reduce-scatter.8.cloned.1.call-update
  318.8 135.9 %reduce-scatter.8.cloned.1.call-done = bf16[512,3584]{1,0:T(8,128)(2,1)} async-done(((bf16[2048,3584]{1,0:T(8,128)(2,1)}), bf16[512,3584]{1,0:T(8,128)(2,1)}) %reduce-scatter.8.cloned.1.call-update) | async-done | bytes 3670032 | tf_op jit(solution)/shard_map/reduce_scatter | solution.py:48
  454.7 6.0 %convert_element_type.33 = f32[512,3584]{1,0:T(8,128)} convert(bf16[512,3584]{1,0:T(8,128)(2,1)} %reduce-scatter.8.cloned.1.call-done) | non-fusion elementwise | flops 1835008 | bytes 11010048 | tf_op jit(solution)/shard_map/convert_element_type | solution.py:55
Async XLA Ops:
  7.4 23.4 %copy-start = (bf16[64,3584]{1,0:T(8,128)(2,1)S(1)}, bf16[64,3584]{1,0:T(8,128)(2,1)}, u32[]{:S(2)}) copy-start(bf16[64,3584]{1,0:T(8,128)(2,1)} %param.5) | copy-start | bytes 1376260
  7.4 23.4 %all-gather.6.cloned.1.call-start = ((), (), s32[]{:S(2)}) async-start(), calls=%async_computation.3 | async-start | bytes 11010048 | tf_op jit(solution)/shard_map/all_gather | solution.py:28
  8.1 27.9 %copy-start.1 = (bf16[256,512]{1,0:T(8,128)(2,1)S(1)}, bf16[256,512]{1,0:T(8,128)(2,1)}, u32[]{:S(2)}) copy-start(bf16[256,512]{1,0:T(8,128)(2,1)} %param.8) | copy-start | bytes 786436
  8.1 27.9 %copy-start.2 = (bf16[128,256]{1,0:T(8,128)(2,1)S(1)}, bf16[128,256]{1,0:T(8,128)(2,1)}, u32[]{:S(2)}) copy-start(bf16[128,256]{1,0:T(8,128)(2,1)} %param.6) | copy-start | bytes 196612
  8.1 49.0 %reduce-scatter.4.cloned.1.call-start = ((), (), s32[]{:S(2)}) async-start(), calls=%async_computation.4 | async-start | bytes 163840 | tf_op jit(solution)/shard_map/reduce_scatter | solution.py:30
  35.9 156.7 %copy-start.3 = (f32[256,512]{1,0:T(8,128)S(1)}, f32[256,512]{1,0:T(8,128)}, u32[]{:S(2)}) copy-start(f32[256,512]{1,0:T(8,128)} %param.9) | copy-start | bytes 1572868
  35.9 79.9 %all-gather.12.cloned.1.call-start = ((), (), s32[]{:S(2)}) async-start(), calls=%async_computation.9 | async-start | bytes 4456448 | tf_op jit(solution)/shard_map/all_gather | solution.py:10
  36.9 155.7 %all-gather.8.cloned.1.call-start = ((), (), s32[]{:S(2)}) async-start(), calls=%async_computation.5 | async-start | bytes 4456448 | tf_op jit(solution)/shard_map/all_gather | solution.py:39
  37.5 175.9 %reduce-scatter.6.cloned.1.call-start = ((), (), s32[]{:S(2)}) async-start(), calls=%async_computation.6 | async-start | bytes 3145728 | tf_op jit(solution)/shard_map/reduce_scatter | solution.py:43
  204.9 91.8 %all-gather.10.cloned.1.call-start = ((), (), s32[]{:S(2)}) async-start(), calls=%async_computation.7 | async-start | bytes 5242880 | tf_op jit(solution)/shard_map/all_gather | solution.py:47
  213.5 241.2 %reduce-scatter.8.cloned.1.call-start = ((), (), s32[]{:S(2)}) async-start(), calls=%async_computation.8 | async-start | bytes 18350080 | tf_op jit(solution)/shard_map/reduce_scatter | solution.py:48
Sparse Core Ops, SparseCore 0:
  9.7 21.0 all-gather.5
  36.0 21.0 reduce-scatter.3
  205.0 8.3 reduce-scatter.5
  214.8 81.8 all-gather.9
Sparse Core Ops, SparseCore 1:
  39.2 76.6 all-gather.11
  118.5 74.0 all-gather.7
  318.8 135.8 reduce-scatter.7
